TPU v7x, 32 devices: a whole 2x2x4 slice. The times are simulated.
32 devices in a mesh: frow: 4 (over z), fcol: 4 (over x, core), chan: 2 (over y).
Axes of the slice: x: 2, y: 2, z: 4, core: 2. Of those that a mesh axis runs over, the one named last changes fastest.
Arguments:
- image_cube: float32 [32, 256, 1024], P('chan', 'frow', 'fcol'), may hold values from -40 to 40
- weights: float32 [3, 256, 1024], P(None, 'frow', 'fcol'), may hold values from 0.5 to 2
Outputs:
- backprojected: float32 [32, 256, 1024], P('chan', 'frow', 'fcol')
- lowrank: float32 [32, 256, 1024], P('chan', 'frow', 'fcol')
All inputs are finite; a program needn't handle non-finite values.
Results may differ from a plain program's by a relative error of at most 0.0003.
Values sent between devices are 32-bit elements; how exact they have to be, the bound alone decides.
A program may use at most 128 MiB of HBM per device.

v0:
```python
import math

import jax
import jax.numpy as jnp
import numpy as np
from jax import lax
from jax.sharding import PartitionSpec as P

JSWEEPS = 3


filter_taps = (0.0625, 0.25, 0.375, 0.25, 0.0625)
band_levels = (12.0, 4.0, 2.5)
rank_level = 2.0
tiny_value = 1e-30


def padded(x, sides, width):
    for axis, dim in sides:
        peers, length = (lax.axis_size(axis), x.shape[dim])
        up = [(i, (i + 1) % peers) for i in range(peers - 1)]
        down = [(j, i) for i, j in up]
        last = lax.slice_in_dim(x, length - width, length, axis=dim)
        leading = lax.slice_in_dim(x, 0, width, axis=dim)
        before = lax.ppermute(last, axis, up)
        after = lax.ppermute(leading, axis, down)
        x = jnp.concatenate([before, x, after], axis=dim)
    return x


def smooth(extended, dilation):
    reach_cells = 2 * dilation
    row_count = extended.shape[-2] - 2 * reach_cells
    col_count = extended.shape[-1] - 2 * reach_cells
    across = filter_taps[0] * extended[..., 0:row_count, :]
    for tap_index in range(1, 5):
        offset = tap_index * dilation
        across = across + filter_taps[tap_index] * extended[..., offset : offset + row_count, :]
    result = filter_taps[0] * across[..., 0:col_count]
    for tap_index in range(1, 5):
        offset = tap_index * dilation
        result = result + filter_taps[tap_index] * across[..., offset : offset + col_count]
    return result


def tournament(order_size):
    players = list(range(order_size))
    tables = []
    for round_index in range(order_size - 1):
        first_list = []
        second_list = []
        for slot_index in range(order_size // 2):
            left_one = players[slot_index]
            right_one = players[order_size - 1 - slot_index]
            first_list.append(min(left_one, right_one))
            second_list.append(max(left_one, right_one))
        order_list = np.array(first_list + second_list, np.int32)
        inverse_list = np.argsort(order_list).astype(np.int32)
        tables.append(
            (
                np.array(first_list, np.int32),
                np.array(second_list, np.int32),
                order_list,
                inverse_list,
            )
        )
        players = [players[0], players[-1]] + players[1:-1]
    return tables


def jacobi(gram_matrix):
    order_size = gram_matrix.shape[0]
    half_size = order_size // 2
    tables = tournament(order_size)
    identity_matrix = jnp.eye(order_size, dtype=gram_matrix.dtype)

    def one_round(matrix, vectors, first_list, second_list, order_list, inverse_list):
        diag_values = jnp.diagonal(matrix)
        left_diag = diag_values[first_list]
        right_diag = diag_values[second_list]
        cross_term = matrix[first_list, second_list]
        gap_value = right_diag - left_diag
        sign_part = jnp.where(gap_value >= 0, 1.0, -1.0)
        tangent = (
            sign_part
            * 2.0
            * cross_term
            / (
                jnp.abs(gap_value)
                + jnp.sqrt(gap_value * gap_value + 4.0 * cross_term * cross_term)
                + tiny_value
            )
        )
        cosine = 1.0 / jnp.sqrt(1.0 + tangent * tangent)
        sine_part = tangent * cosine

        def turn_columns(block):
            placed = block[:, order_list]
            left_cols = placed[:, :half_size]
            right_cols = placed[:, half_size:]
            turned = jnp.concatenate(
                [
                    cosine * left_cols - sine_part * right_cols,
                    sine_part * left_cols + cosine * right_cols,
                ],
                axis=1,
            )
            return turned[:, inverse_list]

        matrix = turn_columns(matrix)
        matrix = turn_columns(matrix.T).T
        vectors = turn_columns(vectors)
        return (matrix, vectors)

    def sweep(counter, carried):
        matrix, vectors = carried
        for first_list, second_list, order_list, inverse_list in tables:
            matrix, vectors = one_round(
                matrix, vectors, first_list, second_list, order_list, inverse_list
            )
        return (matrix, vectors)

    matrix, vectors = lax.fori_loop(0, JSWEEPS, sweep, (gram_matrix, identity_matrix))
    return (jnp.diagonal(matrix), vectors)


def spectral_map(gram_matrix, threshold):
    values, vectors = jacobi(gram_matrix)
    factors = 1.0 - threshold / jnp.sqrt(jnp.maximum(values, threshold * threshold))
    return jnp.dot(vectors * factors[None, :], vectors.T, precision=lax.Precision.HIGHEST)


def shards(image_cube, weights):
    local_channels, row_count, col_count = image_cube.shape
    highest = lax.Precision.HIGHEST
    row_start = lax.axis_index("frow") * row_count
    col_start = lax.axis_index("fcol") * col_count
    total_rows = row_count * lax.axis_size("frow")
    total_cols = col_count * lax.axis_size("fcol")

    def inside(margin):
        row_places = row_start - margin + jnp.arange(row_count + 2 * margin, dtype=jnp.int32)
        col_places = col_start - margin + jnp.arange(col_count + 2 * margin, dtype=jnp.int32)
        row_valid = (row_places >= 0) & (row_places < total_rows)
        col_valid = (col_places >= 0) & (col_places < total_cols)
        return (row_valid[:, None] & col_valid[None, :]).astype(jnp.float32)

    extended = padded(image_cube, (("frow", 1), ("fcol", 2)), 6)
    wide_one = smooth(extended, 1) * inside(4)
    coarse_one = wide_one[:, 4:-4, 4:-4]
    coarse_two = smooth(wide_one, 2)
    band_list = (image_cube - coarse_one, coarse_one - coarse_two, coarse_two)
    squares = jnp.stack([jnp.sum(band * band, axis=0) for band in band_list])
    totals = lax.psum(squares, "chan")
    levels = jnp.asarray(band_levels, jnp.float32)[:, None, None] * weights
    factors = levels / jnp.sqrt(jnp.maximum(totals, levels * levels))
    dual_list = [band_list[band_index] * factors[band_index] for band_index in range(3)]
    stacked = jnp.stack([dual_list[1] - dual_list[0], dual_list[2] - dual_list[1]])
    wide = padded(stacked, (("frow", 2), ("fcol", 3)), 6)
    inner_wide = smooth(wide[1], 2)
    summed_wide = (wide[0][:, 4:-4, 4:-4] + inner_wide) * inside(2)
    backprojected = dual_list[0] + smooth(summed_wide, 1)
    pixels = row_count * col_count
    threshold = rank_level * math.sqrt(pixels)
    flat_cube = image_cube.reshape(local_channels, pixels)
    gathered = lax.all_gather(flat_cube, "chan", axis=0, tiled=True)
    mixing = spectral_map(jnp.dot(gathered, gathered.T, precision=highest), threshold)
    own_rows = lax.dynamic_slice_in_dim(
        mixing, lax.axis_index("chan") * local_channels, local_channels, 0
    )
    lowrank = jnp.dot(own_rows, gathered, precision=highest)
    return (backprojected, lowrank.reshape(image_cube.shape))


def solution(mesh):
    placed = (P("chan", "frow", "fcol"), P(None, "frow", "fcol"))
    return jax.shard_map(
        shards,
        mesh=mesh,
        in_specs=placed,
        out_specs=(P("chan", "frow", "fcol"), P("chan", "frow", "fcol")),
        check_vma=False,
    )
```

profile of v0, /device:TPU:1, one launch (start us, length us, event | category | flops | bytes accessed | tf_op | source)
XLA Modules:
  0.0 757.6 jit_solution(17918893660464054311)
XLA Ops:
  8.2 4.0 collective-permute-start
  13.6 2.5 copy.700
  16.2 2.4 copy.697
  18.7 2.4 copy.699
  22.2 4.3 collective-permute-start.2
  26.5 1.9 collective-permute-start.3
  28.6 3.4 collective-permute-done.3
  33.1 2.3 fusion.161
  36.0 2.3 fusion.165
  38.3 3.2 multiply_reduce_fusion.2
  42.6 1.6 copy.709
  44.4 24.4 %all-reduce.2.cloned.1.call-done = f32[3,64,256]{1,2,0:T(8,128)} async-done(((f32[3,64,256]{1,2,0:T(8,128)}), f32[3,64,256]{1,2,0:T(8,128)}) %all-reduce.2.cloned.1.call-update) | async-done | bytes 196624 | tf_op jit(solution)/shard_map/psum | solution.py:154
  70.0 3.2 subtract_bitcast_fusion.1
  73.2 4.6 slice_maximum_fusion
  77.8 3.8 copy.702
  81.6 3.1 collective-permute-start.4
  84.7 3.6 copy.703
  88.4 1.3 collective-permute-start.5
  89.8 3.5 copy.704
  93.3 2.4 collective-permute-done.5
  95.7 3.5 copy.705
  99.2 1.4 pad_maximum_fusion.100
  100.6 5.1 collective-permute-start.6
  105.8 2.3 collective-permute-start.7
  108.6 3.1 collective-permute-done.7
  111.7 2.6 pad_maximum_fusion.93
  114.6 2.3 fusion.157
  117.8 2.3 fusion.174
  120.0 2.1 fusion.185
  122.2 3.5 copy.706
  125.9 4.1 fusion.239
  130.3 616.8 %while.15 = (s32[]{:T(128)}, f32[32,32]{1,0:T(8,128)S(1)}, f32[32,32]{0,1:T(8,128)S(1)}, s32[]{:T(128)}, s32[32]{0:T(128)S(1)}, /*index=5*/s32[16]{0:T(128)S(1)}...) while((s32[]{:T(128)}, f32[32,32]{1,0:T(8,128)S(1)}, ...), condition=%wide.region_5.6_spmd.clone.clone.clone, body=%wide.region_4.5_spmd.sunk.clone.clone.clone.sunk | while | flops 513938 | bytes 4194541 | solution.py:123
  (3018 shorter events, 620.8 us)
Async XLA Ops:
  7.2 61.7 %all-reduce.2.cloned.1.call-start = ((), (), s32[]{:S(2)}) async-start(), calls=%async_computation | async-start | bytes 786432 | tf_op jit(solution)/shard_map/psum | solution.py:154
  8.2 8.0 %collective-permute-start = (f32[16,6,256]{2,0,1:T(8,128)S(1)}, f32[16,6,256]{2,0,1:T(8,128)S(1)}, u32[]{:S(2)}, u32[]{:S(2)}) collective-permute-start(f32[16,6,256]{2,0,1:T(8,128)S(1)} %copy.707), channel_id=1, source_target_pairs={{0,8},{8,16},{16,24},{1,9},{9,17},{17,25},{2,10},{10,18},{18,26},{... | collective-permute-start | bytes 294920 | tf_op jit(solution)/shard_map/ppermute | solution.py:25
  12.3 6.3 collective-permute-start.1
  16.2 15.8 %copy-start = (f32[16,64,256]{1,0,2:T(8,128)}, f32[16,64,256]{1,0,2:T(8,128)S(1)}, u32[]{:S(2)}) copy-start(f32[16,64,256]{1,0,2:T(8,128)S(1)} %copy.700) | copy-start | bytes 3145732
  21.1 10.8 %copy-start.10 = (f32[16,6,256]{1,0,2:T(8,128)S(1)}, f32[16,6,256]{1,0,2:T(8,128)}, u32[]{:S(2)}) copy-start(f32[16,6,256]{1,0,2:T(8,128)} %copy.697) | copy-start | bytes 294916
  21.1 10.8 %copy-start.11 = (f32[16,6,256]{1,0,2:T(8,128)S(1)}, f32[16,6,256]{1,0,2:T(8,128)}, u32[]{:S(2)}) copy-start(f32[16,6,256]{1,0,2:T(8,128)} %copy.699) | copy-start | bytes 294916
  22.2 6.3 collective-permute-start.2
  26.5 5.4 collective-permute-start.3
  42.3 26.5 %copy-start.165 = (f32[3]{0:T(128)S(1)}, f32[3]{0:T(128)}, u32[]{:S(2)}) copy-start(f32[3]{0:T(128)} %constant.406.clone) | copy-start | bytes 40
  42.3 83.6 %all-gather.2.cloned.1.call-start = ((), (), s32[]{:S(2)}) async-start(), calls=%async_computation.1 | async-start | bytes 3145728 | tf_op jit(solution)/shard_map/all_gather | solution.py:166
  81.6 8.1 %collective-permute-start.4 = (f32[2,16,6,256]{3,1,2,0:T(8,128)S(1)}, f32[2,16,6,256]{3,1,2,0:T(8,128)S(1)}, u32[]{:S(2)}, u32[]{:S(2)}) collective-permute-start(f32[2,16,6,256]{3,1,2,0:T(8,128)S(1)} %copy.702), channel_id=1, source_target_pairs={{0,8},{8,16},{16,24},{1,9},{9,17},{17,25},{2,10},{10,18},{18,26},{... | collective-permute-start | bytes 589832 | tf_op jit(solution)/shard_map/ppermute | solution.py:25
  88.4 7.3 collective-permute-start.5
  99.2 12.5 %copy-start.3 = (f32[2,16,6,256]{2,1,3,0:T(8,128)S(1)}, f32[2,16,6,256]{2,1,3,0:T(8,128)}, u32[]{:S(2)}) copy-start(f32[2,16,6,256]{2,1,3,0:T(8,128)} %copy.704) | copy-start | bytes 589828
  99.2 12.5 %copy-start.4 = (f32[2,16,6,256]{2,1,3,0:T(8,128)S(1)}, f32[2,16,6,256]{2,1,3,0:T(8,128)}, u32[]{:S(2)}) copy-start(f32[2,16,6,256]{2,1,3,0:T(8,128)} %copy.705) | copy-start | bytes 589828
  99.2 12.5 %copy-start.6 = (f32[1,16,64,256]{2,1,3,0:T(8,128)S(1)}, f32[1,16,64,256]{2,1,3,0:T(8,128)}, u32[]{:S(2)}) copy-start(f32[1,16,64,256]{2,1,3,0:T(8,128)} %copy-done.5) | copy-start | bytes 3145732
  99.2 12.5 %copy-start.8 = (f32[1,16,64,256]{2,1,3,0:T(8,128)S(1)}, f32[1,16,64,256]{2,1,3,0:T(8,128)}, u32[]{:S(2)}) copy-start(f32[1,16,64,256]{2,1,3,0:T(8,128)} %copy-done.7) | copy-start | bytes 3145732
  100.6 8.0 %collective-permute-start.6 = (f32[2,16,76,6]{2,1,3,0:T(8,128)S(1)}, f32[2,16,76,6]{2,1,3,0:T(8,128)S(1)}, u32[]{:S(2)}, u32[]{:S(2)}) collective-permute-start(f32[2,16,76,6]{2,1,3,0:T(8,128)S(1)} %get-tuple-element.3668), channel_id=1, source_target_pairs={{0,2},{2,4},{4,6},{1,3},{3,5},{5,7},{8,10},{10,12},{12,14},{9,11},... | collective-permute-start | bytes 175112 | tf_op jit(solution)/shard_map/ppermute | solution.py:25
  105.8 5.9 collective-permute-start.7
  130.3 616.9 %copy-start.43 = (s32[32]{0:T(128)S(1)}, s32[32]{0:T(128)}, u32[]{:S(2)}) copy-start(s32[32]{0:T(128)} %or_bitcast_fusion.1) | copy-start | bytes 388
  130.3 617.9 %copy-start.9 = (f32[32,16384]{1,0:T(8,128)S(1)}, f32[32,16384]{1,0:T(8,128)}, u32[]{:S(2)}) copy-start(f32[32,16384]{1,0:T(8,128)} %all-gather.2.cloned.1.call-done) | copy-start | bytes 6291460
  193.1 9.8 %copy-start.87 = (s32[32]{0:T(128)S(1)}, s32[32]{0:T(128)}, u32[]{:S(2)}) copy-start(s32[32]{0:T(128)} %get-tuple-element.4569) | copy-start | bytes 388 | tf_op jit(solution)/shard_map/while
  199.7 9.8 %copy-start.91 = (s32[32]{0:T(128)S(1)}, s32[32]{0:T(128)}, u32[]{:S(2)}) copy-start(s32[32]{0:T(128)} %get-tuple-element.4574) | copy-start | bytes 388 | tf_op jit(solution)/shard_map/while
  206.4 9.8 %copy-start.95 = (s32[32]{0:T(128)S(1)}, s32[32]{0:T(128)}, u32[]{:S(2)}) copy-start(s32[32]{0:T(128)} %get-tuple-element.4579) | copy-start | bytes 388 | tf_op jit(solution)/shard_map/while
  213.0 9.8 %copy-start.99 = (s32[32]{0:T(128)S(1)}, s32[32]{0:T(128)}, u32[]{:S(2)}) copy-start(s32[32]{0:T(128)} %get-tuple-element.4584) | copy-start | bytes 388 | tf_op jit(solution)/shard_map/while
  398.6 9.8 %copy-start.87 = (s32[32]{0:T(128)S(1)}, s32[32]{0:T(128)}, u32[]{:S(2)}) copy-start(s32[32]{0:T(128)} %get-tuple-element.4569) | copy-start | bytes 388 | tf_op jit(solution)/shard_map/while
  405.3 9.8 %copy-start.91 = (s32[32]{0:T(128)S(1)}, s32[32]{0:T(128)}, u32[]{:S(2)}) copy-start(s32[32]{0:T(128)} %get-tuple-element.4574) | copy-start | bytes 388 | tf_op jit(solution)/shard_map/while
  411.9 9.8 %copy-start.95 = (s32[32]{0:T(128)S(1)}, s32[32]{0:T(128)}, u32[]{:S(2)}) copy-start(s32[32]{0:T(128)} %get-tuple-element.4579) | copy-start | bytes 388 | tf_op jit(solution)/shard_map/while
  418.6 9.8 %copy-start.99 = (s32[32]{0:T(128)S(1)}, s32[32]{0:T(128)}, u32[]{:S(2)}) copy-start(s32[32]{0:T(128)} %get-tuple-element.4584) | copy-start | bytes 388 | tf_op jit(solution)/shard_map/while
  604.2 9.8 %copy-start.87 = (s32[32]{0:T(128)S(1)}, s32[32]{0:T(128)}, u32[]{:S(2)}) copy-start(s32[32]{0:T(128)} %get-tuple-element.4569) | copy-start | bytes 388 | tf_op jit(solution)/shard_map/while
  610.8 9.8 %copy-start.91 = (s32[32]{0:T(128)S(1)}, s32[32]{0:T(128)}, u32[]{:S(2)}) copy-start(s32[32]{0:T(128)} %get-tuple-element.4574) | copy-start | bytes 388 | tf_op jit(solution)/shard_map/while
  617.5 9.8 %copy-start.95 = (s32[32]{0:T(128)S(1)}, s32[32]{0:T(128)}, u32[]{:S(2)}) copy-start(s32[32]{0:T(128)} %get-tuple-element.4579) | copy-start | bytes 388 | tf_op jit(solution)/shard_map/while
  624.1 9.8 %copy-start.99 = (s32[32]{0:T(128)S(1)}, s32[32]{0:T(128)}, u32[]{:S(2)}) copy-start(s32[32]{0:T(128)} %get-tuple-element.4584) | copy-start | bytes 388 | tf_op jit(solution)/shard_map/while
  (401 other events, 3275.1 us)
Sparse Core Ops, SparseCore 0:
  42.5 26.3 all-reduce.1
  70.9 33.0 all-gather.1
where the time goes:
time: 765 us; the launch traced here: 758 us
  local copies, waits for them, and re-layouts  618 us (81%)
  other arithmetic  53.1 us (7%)
  waiting for transfers between devices  33.3 us (4%)
  starting transfers between devices  23.6 us (3%)
  between operations  15 us (2%)
  loops' own time  9.12 us (1%)
    gather x462, local copies, waits for them, and re-layouts, turn_columns(): return turned[:, inverse_list]  173 us
    gather x279, local copies, waits for them, and re-layouts, turn_columns(): placed = block[:, order_list]  160 us
    gather x93, local copies, waits for them, and re-layouts, one_round(): diag_values = jnp.diagonal(matrix)  66.6 us
    gather x93, local copies, waits for them, and re-layouts, one_round(): cross_term = matrix[first_list, second_list]  62 us
    gather x93, local copies, waits for them, and re-layouts, one_round(): left_diag = diag_values[first_list]  61.1 us
    gather x93, local copies, waits for them, and re-layouts, one_round(): right_diag = diag_values[second_list]  61.1 us
    psum x1, waiting for transfers between devices, shards(): totals = lax.psum(squares, 'chan')  24.4 us
    ppermute x4, starting transfers between devices, padded(): before = lax.ppermute(last, axis, up)  16.5 us
  transfers between devices with their start and end apart: 10, of which 4 were waited for; matrix products, arithmetic and copies ran while one was open for 6% of the time, Pallas kernels for 0%

commit v1 on v0

v1 whole, which is shorter than its diff:
```python
import functools
import math

import jax
import jax.numpy as jnp
from jax import lax
from jax.experimental import pallas as pl
from jax.experimental.pallas import tpu as pltpu
from jax.sharding import PartitionSpec as P

JSWEEPS = 3


filter_taps = (0.0625, 0.25, 0.375, 0.25, 0.0625)
band_levels = (12.0, 4.0, 2.5)
rank_level = 2.0
tiny_value = 1e-30


def rank_round(state, marks):
    quads, sides, labels, cosine, sine = state
    eye, lane, row, first_mask, last_mask, step_mask, last = marks
    upper_left, upper_right, lower_left, lower_right = quads
    side_top, side_bottom = sides
    label_top, label_bottom = labels

    def across(values):
        return jnp.sum(jnp.where(eye, values, 0.0), axis=0, keepdims=True)

    cosine_row = across(cosine)
    sine_row = across(sine)

    def turn_rows(top, bottom):
        return cosine * top - sine * bottom, sine * top + cosine * bottom

    def move_rows(top, bottom):
        up = pltpu.roll(jnp.where(row == 0, bottom, top), 1, 0)
        down = pltpu.roll(bottom, last, 0)
        return jnp.where(row == 0, top, up), jnp.where(row == last, top, down)

    def turn_cols(left, right):
        return cosine_row * left - sine_row * right, sine_row * left + cosine_row * right

    def move_cols(left, right):
        ahead = pltpu.roll(jnp.where(lane == 0, right, left), 1, 1)
        back = pltpu.roll(right, lane.shape[1] - 1, 1)
        return jnp.where(lane == 0, left, ahead), jnp.where(lane == last, left, back)

    upper_left, lower_left = move_rows(*turn_rows(upper_left, lower_left))
    upper_right, lower_right = move_rows(*turn_rows(upper_right, lower_right))
    upper_left, upper_right = turn_cols(upper_left, upper_right)
    lower_left, lower_right = turn_cols(lower_left, lower_right)
    sides = move_rows(*turn_rows(side_top, side_bottom))
    label_top, label_bottom = move_rows(label_top, label_bottom)
    own_top = jnp.where(step_mask, upper_left, jnp.where(first_mask, upper_right, 0.0))
    next_mask = lane == row + 1
    own_bottom = jnp.where(
        next_mask & (row < last), lower_right, jnp.where(last_mask, lower_left, 0.0)
    )
    pair = jnp.where(next_mask & (row < last), upper_right, jnp.where(last_mask, upper_left, 0.0))
    gap = jnp.sum(own_bottom - own_top, axis=1, keepdims=True)
    cross = jnp.sum(pair, axis=1, keepdims=True)
    cosine, sine = turn_of(gap, cross, label_top < label_bottom)
    upper = move_cols(upper_left, upper_right)
    lower = move_cols(lower_left, lower_right)
    return (upper + lower, sides, (label_top, label_bottom), cosine, sine)


def turn_of(gap, cross, ordered):
    gap = jnp.broadcast_to(gap, ordered.shape)
    cross = jnp.broadcast_to(cross, ordered.shape)
    positive = (gap > 0) | ((gap == 0) & ordered)
    double = 2.0 * cross
    root = jnp.sqrt(gap * gap + double * double)
    tangent = jnp.where(positive, double, -double) / (jnp.abs(gap) + root + tiny_value)
    cosine = lax.rsqrt(1.0 + tangent * tangent)
    return cosine, tangent * cosine


def rank_start(gram):
    order = gram.shape[0]
    half, last, lanes = order // 2, order // 2 - 1, 128
    highest = lax.Precision.HIGHEST
    row = lax.broadcasted_iota(jnp.int32, (half, lanes), 0)
    lane = lax.broadcasted_iota(jnp.int32, (half, lanes), 1)
    eye = lane == row
    first_mask = (row == 1) & (lane == 0)
    last_mask = (row == last) & (lane == last)
    step_mask = ((row == 0) & (lane == 0)) | ((row >= 2) & (lane == row - 1))
    marks = (eye, lane, row, first_mask, last_mask, step_mask, last)
    mirror = lane == order - 1 - row
    pick_row = lax.broadcasted_iota(jnp.int32, (order, lanes), 0)
    pick_lane = lax.broadcasted_iota(jnp.int32, (order, lanes), 1)
    one = lambda mask: jnp.where(mask, 1.0, 0.0)
    pick_left = one((pick_row == pick_lane) & (pick_lane < half))
    pick_right = one((pick_row == order - 1 - pick_lane) & (pick_lane < half))
    dot = functools.partial(jnp.dot, precision=highest, preferred_element_type=jnp.float32)
    flip_row = lax.broadcasted_iota(jnp.int32, (half, half), 0)
    flip_lane = lax.broadcasted_iota(jnp.int32, (half, half), 1)
    flip = one(flip_row + flip_lane == last)
    top, bottom = gram[:half], dot(flip, gram[half:])
    quads = (dot(top, pick_left), dot(top, pick_right), dot(bottom, pick_left), dot(bottom, pick_right))
    sides = (one(eye), one(mirror))
    labels = (row, order - 1 - row)
    total = lambda values: jnp.sum(jnp.where(eye, values, 0.0), axis=1, keepdims=True)
    cosine, sine = turn_of(
        total(quads[3] - quads[0]), total(quads[1]), labels[0] < labels[1]
    )
    return (quads, sides, labels, cosine, sine), marks


def rank_finish(state, marks, threshold):
    highest = lax.Precision.HIGHEST
    eye = marks[0]
    total = lambda values: jnp.sum(jnp.where(eye, values, 0.0), axis=1, keepdims=True)
    quads, sides = state[0], state[1]
    mixing = 0.0
    for quad, side in zip((quads[0], quads[3]), sides):
        values = total(quad)
        factor = 1.0 - threshold / jnp.sqrt(jnp.maximum(values, threshold * threshold))
        mixing = mixing + lax.dot_general(
            side * factor, side, (((0,), (0,)), ((), ())), precision=highest,
            preferred_element_type=jnp.float32,
        )
    order = 2 * eye.shape[0]
    return mixing[:order, :order]


def spread(x, dilation):
    for axis in (0, 1):
        size = x.shape[axis]
        total = filter_taps[2] * x
        for step in (1, 2):
            shift = step * dilation
            near = pltpu.roll(x, shift, axis) + pltpu.roll(x, size - shift, axis)
            total = total + filter_taps[2 - step] * near
        x = total
    return x


def split_two(values):
    high = values.astype(jnp.bfloat16)
    low = (values - high.astype(jnp.float32)).astype(jnp.bfloat16)
    return high, low


def facet_kernel(
    threshold, image_ref, flat_ref, weights_ref, back_ref, rank_ref,
    wide, bands, sums, other_sums, diffs, full, gram, other_gram, mixing,
    pack_out, pack_in, pack_out_two, pack_in_two, send_sems, recv_sems, local_sems,
):
    channels, rows, cols = image_ref.shape
    pixels = rows * cols
    part = pixels // 2
    names = ("frow", "fcol", "chan")
    place = {name: lax.axis_index(name) for name in names}
    count = {name: lax.axis_size(name) for name in names}
    me = place["chan"]
    partner = 1 - me
    has = {
        ("frow", 1): place["frow"] < count["frow"] - 1,
        ("frow", -1): place["frow"] > 0,
        ("fcol", 1): place["fcol"] < count["fcol"] - 1,
        ("fcol", -1): place["fcol"] > 0,
    }
    barrier = pltpu.get_barrier_semaphore()
    mesh_ids = pl.DeviceIdType.MESH

    def target(name, step):
        ids = dict(place)
        ids[name] = place[name] + step
        return tuple(ids[key] for key in names)

    def mate():
        return (place["frow"], place["fcol"], partner)

    def copy_to(index, source, sink, device):
        return pltpu.make_async_remote_copy(
            src_ref=source, dst_ref=sink, send_sem=send_sems.at[index],
            recv_sem=recv_sems.at[index], device_id=device, device_id_type=mesh_ids,
        )

    own_rows = pl.ds(pl.multiple_of(me * channels, channels), channels)
    to_mate = pl.ds(pl.multiple_of(partner * part, part), part)
    to_self = pl.ds(pl.multiple_of(me * part, part), part)
    keep_flat = pltpu.make_async_copy(flat_ref, full.at[own_rows, :], local_sems.at[0])
    keep_image = pltpu.make_async_copy(
        image_ref, wide.at[:, pl.ds(8, rows), :], local_sems.at[1]
    )
    keep_flat.start()
    keep_image.start()

    zero_rows = jnp.zeros((channels, 8, cols), jnp.float32)

    @pl.when(jnp.logical_not(has["frow", -1]))
    def _():
        wide[:, 0:8, :] = zero_rows
        diffs[0, :, 0:8, :] = zero_rows
        diffs[1, :, 0:8, :] = zero_rows

    @pl.when(jnp.logical_not(has["frow", 1]))
    def _():
        wide[:, rows + 8 : rows + 16, :] = zero_rows
        diffs[0, :, rows + 8 : rows + 16, :] = zero_rows
        diffs[1, :, rows + 8 : rows + 16, :] = zero_rows

    for side, step in ((0, -1), (1, 1)):

        @pl.when(jnp.logical_not(has["fcol", step]))
        def _(side=side):
            pack_in[side] = jnp.zeros(pack_in.shape[1:], jnp.float32)
            pack_in_two[side] = jnp.zeros(pack_in_two.shape[1:], jnp.float32)

    pl.semaphore_signal(barrier, inc=1, device_id=mate(), device_id_type=mesh_ids)
    friends = 1
    for key in has:

        @pl.when(has[key])
        def _(key=key):
            pl.semaphore_signal(barrier, inc=1, device_id=target(*key), device_id_type=mesh_ids)

        friends = friends + jnp.where(has[key], 1, 0)
    pl.semaphore_wait(barrier, friends)

    first_part = copy_to(0, flat_ref.at[:, to_mate], full.at[own_rows, to_mate], mate())
    second_part = copy_to(1, flat_ref.at[:, to_self], full.at[own_rows, to_self], mate())
    below = lambda ref, at: ref.at[..., pl.ds(at, 8), :]

    def row_copies(index, source, offset, sink):
        return (
            (("frow", 1), ("frow", -1), copy_to(
                index, below(source, offset + rows - 8), below(sink, 0), target("frow", 1))),
            (("frow", -1), ("frow", 1), copy_to(
                index + 1, below(source, offset), below(sink, rows + 8), target("frow", -1))),
        )

    def col_copies(index, source, sink):
        return (
            (("fcol", 1), ("fcol", -1), copy_to(
                index, source.at[1], sink.at[0], target("fcol", 1))),
            (("fcol", -1), ("fcol", 1), copy_to(
                index + 1, source.at[0], sink.at[1], target("fcol", -1))),
        )

    def start_all(copies):
        for goes, _, copy in copies:

            @pl.when(has[goes])
            def _(copy=copy):
                copy.start()

    def arrive_all(copies):
        for _, comes, copy in copies:

            @pl.when(has[comes])
            def _(copy=copy):
                copy.wait_recv()

    def left_all(copies):
        for goes, _, copy in copies:

            @pl.when(has[goes])
            def _(copy=copy):
                copy.wait_send()

    rows_one = row_copies(2, image_ref, 0, wide)
    cols_one = col_copies(4, pack_out, pack_in)
    rows_two = row_copies(8, diffs, 8, diffs)
    cols_two = col_copies(10, pack_out_two, pack_in_two)
    start_all(rows_one)
    first_part.start()

    tall = rows + 16
    tile_lane = lax.broadcasted_iota(jnp.int32, (tall, 128), 1)

    def pack_edges(load, store):
        def body(ch, sides):
            left, right = sides
            here = (tile_lane >= ch * 8) & (tile_lane < ch * 8 + 8)
            tile_first = pltpu.roll(load(ch, pl.ds(0, 128)), ch * 8, 1)
            tile_last = pltpu.roll(load(ch, pl.ds(cols - 128, 128)), ch * 8 + 8, 1)
            return jnp.where(here, tile_first, left), jnp.where(here, tile_last, right)

        empty = jnp.zeros((tall, 128), jnp.float32)
        left, right = lax.fori_loop(0, channels, body, (empty, empty))
        store(0, left)
        store(1, right)

    def edge_tile(ch, before, after):
        after = pltpu.roll(after, 128 - ch * 8, 1)
        before = pltpu.roll(before, 120 - ch * 8, 1)
        return jnp.where(tile_lane < 8, after, jnp.where(tile_lane >= 120, before, 0.0))

    long = cols + 128
    row_at = lax.broadcasted_iota(jnp.int32, (tall, long), 0) - 8
    col_at = lax.broadcasted_iota(jnp.int32, (tall, long), 1)
    col_at = jnp.where(col_at < cols + 64, col_at, col_at - long)
    row_at = row_at + place["frow"] * rows
    col_at = col_at + place["fcol"] * cols
    valid = (row_at >= 0) & (row_at < count["frow"] * rows)
    valid = valid & (col_at >= 0) & (col_at < count["fcol"] * cols)
    inside = lambda values: jnp.where(valid, values, 0.0)

    keep_image.wait()
    arrive_all(rows_one)
    pack_edges(lambda ch, at: wide[ch, :, at], pack_out.__setitem__)
    start_all(cols_one)
    sums[...] = jnp.zeros(sums.shape, jnp.float32)
    arrive_all(cols_one)

    def analyse(ch, carried):
        center = wide[ch]
        tile = edge_tile(ch, pack_in[0], pack_in[1])
        coarse_one = inside(spread(jnp.concatenate([center, tile], axis=1), 1))
        coarse_two = spread(coarse_one, 2)[8 : rows + 8, :cols]
        coarse_one = coarse_one[8 : rows + 8, :cols]
        for index, band in enumerate(
            (center[8 : rows + 8] - coarse_one, coarse_one - coarse_two, coarse_two)
        ):
            bands[index, ch] = band
            sums[index] = sums[index] + band * band
        return carried

    lax.fori_loop(0, channels, analyse, 0)
    share_sums = copy_to(6, sums, other_sums, mate())

    keep_flat.wait()
    first_part.wait_recv()
    order = 2 * channels
    block = 1024
    start = me * part

    def gram_step(step, total):
        at = pl.ds(pl.multiple_of(start + step * block, block), block)
        both = jnp.concatenate(split_two(full[:, at]), axis=0)
        return total + lax.dot_general(
            both, both, (((1,), (1,)), ((), ())), preferred_element_type=jnp.float32
        )

    product = lax.fori_loop(
        0, part // block, gram_step, jnp.zeros((2 * order, 2 * order), jnp.float32)
    )
    gram[:, :order] = (
        product[:order, :order] + (product[:order, order:] + product[order:, :order])
    ) + product[order:, order:]
    share_gram = copy_to(7, gram, other_gram, mate())
    share_gram.start()

    share_sums.start()
    second_part.start()

    share_gram.wait_recv()
    state, marks = rank_start(gram[:, :order] + other_gram[:, :order])
    rounds = JSWEEPS * (order - 1)
    turn = lambda _, carried: rank_round(carried, marks)
    state = lax.fori_loop(0, 3 * rounds // 10, turn, state)
    share_sums.wait_recv()
    for index in range(3):
        levels = band_levels[index] * weights_ref[index]
        totals = sums[index] + other_sums[index]
        other_sums[index] = levels / jnp.sqrt(jnp.maximum(totals, levels * levels))

    def project(ch, carried):
        duals = [bands[index, ch] * other_sums[index] for index in range(3)]
        back_ref[ch] = duals[0]
        diffs[0, ch, pl.ds(8, rows), :] = duals[1] - duals[0]
        diffs[1, ch, pl.ds(8, rows), :] = duals[2] - duals[1]
        return carried

    lax.fori_loop(0, channels, project, 0)
    start_all(rows_two)
    state = lax.fori_loop(3 * rounds // 10, 8 * rounds // 10, turn, state)
    arrive_all(rows_two)
    for index in range(2):
        pack_edges(
            lambda ch, at, index=index: diffs[index, ch, :, at],
            lambda side, value, index=index: pack_out_two.__setitem__((side, index), value),
        )
    start_all(cols_two)
    state = lax.fori_loop(8 * rounds // 10, rounds, turn, state)
    mixing[:, :order] = rank_finish(state, marks, threshold)

    arrive_all(cols_two)

    def synthesise(ch, carried):
        outer, inner = [
            jnp.concatenate(
                [diffs[index, ch], edge_tile(ch, pack_in_two[0, index], pack_in_two[1, index])],
                axis=1,
            )
            for index in range(2)
        ]
        summed = inside(outer + spread(inner, 2))
        back_ref[ch] = back_ref[ch] + spread(summed, 1)[8 : rows + 8, :cols]
        return carried

    lax.fori_loop(0, channels, synthesise, 0)

    second_part.wait_recv()
    high, low = split_two(mixing[own_rows, :order])
    left = jnp.concatenate([high, high, low, low], axis=1)

    def rank_step(step, carried):
        at = pl.ds(pl.multiple_of(step * block, block), block)
        high, low = split_two(full[:, at])
        right = jnp.concatenate([high, low, high, low], axis=0)
        rank_ref[:, at] = jnp.dot(left, right, preferred_element_type=jnp.float32)
        return carried

    lax.fori_loop(0, pixels // block, rank_step, 0)
    for copies in (rows_one, cols_one, rows_two, cols_two):
        left_all(copies)
    for copy in (first_part, second_part, share_sums, share_gram):
        copy.wait_send()


def shards(image_cube, weights):
    channels, rows, cols = image_cube.shape
    pixels = rows * cols
    threshold = rank_level * math.sqrt(pixels)
    order = channels * lax.axis_size("chan")
    tall = rows + 16
    f32 = jnp.float32
    anywhere = pl.BlockSpec(memory_space=pl.ANY)
    in_vmem = pl.BlockSpec(memory_space=pltpu.VMEM)
    back, rank = pl.pallas_call(
        functools.partial(facet_kernel, threshold),
        out_shape=(
            jax.ShapeDtypeStruct(image_cube.shape, f32),
            jax.ShapeDtypeStruct((channels, pixels), f32),
        ),
        in_specs=[anywhere, anywhere, in_vmem],
        out_specs=(in_vmem, in_vmem),
        scratch_shapes=[
            pltpu.VMEM((channels, tall, cols), f32),
            pltpu.VMEM((3, channels, rows, cols), f32),
            pltpu.VMEM((3, rows, cols), f32),
            pltpu.VMEM((3, rows, cols), f32),
            pltpu.VMEM((2, channels, tall, cols), f32),
            pltpu.VMEM((order, pixels), f32),
            pltpu.VMEM((order, 128), f32),
            pltpu.VMEM((order, 128), f32),
            pltpu.VMEM((order, 128), f32),
            pltpu.VMEM((2, tall, 128), f32),
            pltpu.VMEM((2, tall, 128), f32),
            pltpu.VMEM((2, 2, tall, 128), f32),
            pltpu.VMEM((2, 2, tall, 128), f32),
            pltpu.SemaphoreType.DMA((12,)),
            pltpu.SemaphoreType.DMA((12,)),
            pltpu.SemaphoreType.DMA((2,)),
        ],
        compiler_params=pltpu.CompilerParams(
            collective_id=0, has_side_effects=True, vmem_limit_bytes=50 * 2**20
        ),
    )(image_cube, image_cube.reshape(channels, pixels), weights)
    return back, rank.reshape(image_cube.shape)


def solution(mesh):
    placed = (P("chan", "frow", "fcol"), P(None, "frow", "fcol"))
    return jax.shard_map(
        shards,
        mesh=mesh,
        in_specs=placed,
        out_specs=(P("chan", "frow", "fcol"), P("chan", "frow", "fcol")),
        check_vma=False,
    )
```

time: 765 us -> 57.7 us (0.08)
  local copies, waits for them, and re-layouts: 618 us -> 5.16 us
  other arithmetic: 53.1 us -> 0 us
  Pallas kernels: 0 us -> 51.8 us
  waiting for transfers between devices: 33.3 us -> 0 us
  starting transfers between devices: 23.6 us -> 0 us
  between operations: 15 us -> 0.66 us
  loops' own time: 9.12 us -> 0 us
    gather x1114 -> x0, local copies, waits for them, and re-layouts: 585 us -> none  [the longest x462 173 us: turn_columns(): return turned[:, inverse_list]]
    pallas_call x0 -> x1, Pallas kernels: none -> 51.8 us  [shards(): pl.pallas_call(functools.partial(facet_kernel, threshold), out_shape=(jax...]
    psum x1 -> x0, waiting for transfers between devices: 24.4 us -> none  [shards(): totals = lax.psum(squares, 'chan')]
    ppermute x8 -> x0, starting transfers between devices: 23.3 us -> none  [the longest x4 16.5 us: padded(): before = lax.ppermute(last, axis, up)]
    sub x187 -> x0, other arithmetic: 14.2 us -> none  [the longest x186 14.2 us: turn_columns(): cosine * left_cols - sine_part * right_cols]
    ppermute x4 -> x0, local copies, waits for them, and re-layouts: 11.9 us -> none  [the longest x2 5.96 us: padded(): after = lax.ppermute(leading, axis, down)]
    add x5 -> x0, other arithmetic: 11.3 us -> none  [the longest x4 9.2 us: smooth(): across + filter_taps[tap_index] * extended[..., offset:offset + row_count...]
    another operation x1 -> x0, loops' own time: 9.12 us -> none  [jacobi(): lax.fori_loop(0, JSWEEPS, sweep, (gram_matrix, identity_matrix))]
  transfers between devices with their start and end apart: 10 -> 0, of which waited for: 4 -> 0; matrix products, arithmetic and copies ran while one was open for 6% -> 0% of each run, Pallas kernels for 0% -> 0%
where the time goes in v1:
time: 57.7 us; the launch traced here: 57.6 us
  Pallas kernels  51.8 us (90%)
  local copies, waits for them, and re-layouts  5.16 us (9%)
  between operations  0.66 us (1%)
    pallas_call x1, Pallas kernels, shards(): pl.pallas_call(functools.partial(facet_kernel, threshold), out_shape=(jax...  51.8 us
    unnamed x7, local copies, waits for them, and re-layouts  5.16 us

profile of v1, /device:TPU:1, one launch (start us, length us, event | category | flops | bytes accessed | tf_op | source)
XLA Modules:
  0.0 57.6 jit_solution(7972408601494392644)
XLA Ops:
  0.6 0.0 copy-start
  0.6 0.0 copy-start.1
  0.6 2.9 %copy.4 = f32[2,8,64,256]{3,1,2,0:T(8,128)} copy(f32[2,8,64,256]{3,2,1,0:T(8,128)} %bitcast.4) | data formatting | bytes 2097152
  3.6 0.0 copy-done
  3.6 0.0 copy-done.1
  3.6 51.8 %shard_map.41 = (f32[16,64,256]{2,1,0:T(8,128)S(1)}, f32[16,16384]{1,0:T(8,128)S(1)}) custom-call(f32[16,64,256]{2,1,0:T(8,128)S(1)} %copy-done, f32[16,16384]{1,0:T(8,128)} %bitcast.6, f32[3,64,256]{2,1,0:T(8,128)S(1)} %copy-done.1), custom_call_target="tpu_custom_call" | custom-call | tf_op jit(solution)/shard_map/pallas_call | solution.py:426
  55.3 1.3 %copy.5 = f32[2,8,64,256]{3,2,1,0:T(8,128)} copy(f32[2,8,64,256]{3,1,2,0:T(8,128)S(1)} %bitcast.5) | data formatting | bytes 2097152
  56.6 1.0 %copy.7 = f32[16,64,256]{2,1,0:T(8,128)} copy(f32[16,64,256]{2,1,0:T(8,128)S(1)} %get-tuple-element.8) | data formatting | bytes 2097152
Async XLA Ops:
  0.6 2.9 %copy-start = (f32[16,64,256]{2,1,0:T(8,128)S(1)}, f32[16,64,256]{2,1,0:T(8,128)}, u32[]{:S(2)}) copy-start(f32[16,64,256]{2,1,0:T(8,128)} %image_ref.1) | copy-start | bytes 3145732
  0.6 2.9 %copy-start.1 = (f32[3,64,256]{2,1,0:T(8,128)S(1)}, f32[3,64,256]{2,1,0:T(8,128)}, u32[]{:S(2)}) copy-start(f32[3,64,256]{2,1,0:T(8,128)} %weights_ref.1) | copy-start | bytes 589828

commit v2 on v1

--- a/solution.py
+++ b/solution.py
@@ -129,13 +129,10 @@
 def spread(x, dilation):
     for axis in (0, 1):
         size = x.shape[axis]
-        total = filter_taps[2] * x
-        for step in (1, 2):
-            shift = step * dilation
-            near = pltpu.roll(x, shift, axis) + pltpu.roll(x, size - shift, axis)
-            total = total + filter_taps[2 - step] * near
-        x = total
-    return x
+        pair = x + pltpu.roll(x, 2 * dilation, axis)
+        ends = pair + pltpu.roll(pair, size - 2 * dilation, axis)
+        x = ends + 4.0 * (x + pltpu.roll(pair, size - dilation, axis))
+    return x * (filter_taps[0] * filter_taps[0])
 
 
 def split_two(values):
@@ -145,7 +142,7 @@
 
 
 def facet_kernel(
-    threshold, image_ref, flat_ref, weights_ref, back_ref, rank_ref,
+    threshold, image_ref, weights_ref, back_ref, rank_ref,
     wide, bands, sums, other_sums, diffs, full, gram, other_gram, mixing,
     pack_out, pack_in, pack_out_two, pack_in_two, send_sems, recv_sems, local_sems,
 ):
@@ -183,11 +180,9 @@
     own_rows = pl.ds(pl.multiple_of(me * channels, channels), channels)
     to_mate = pl.ds(pl.multiple_of(partner * part, part), part)
     to_self = pl.ds(pl.multiple_of(me * part, part), part)
-    keep_flat = pltpu.make_async_copy(flat_ref, full.at[own_rows, :], local_sems.at[0])
     keep_image = pltpu.make_async_copy(
-        image_ref, wide.at[:, pl.ds(8, rows), :], local_sems.at[1]
+        image_ref, wide.at[:, pl.ds(8, rows), :], local_sems.at[0]
     )
-    keep_flat.start()
     keep_image.start()
 
     zero_rows = jnp.zeros((channels, 8, cols), jnp.float32)
@@ -222,8 +217,8 @@
         friends = friends + jnp.where(has[key], 1, 0)
     pl.semaphore_wait(barrier, friends)
 
-    first_part = copy_to(0, flat_ref.at[:, to_mate], full.at[own_rows, to_mate], mate())
-    second_part = copy_to(1, flat_ref.at[:, to_self], full.at[own_rows, to_self], mate())
+    first_part = copy_to(0, full.at[own_rows, to_mate], full.at[own_rows, to_mate], mate())
+    second_part = copy_to(1, full.at[own_rows, to_self], full.at[own_rows, to_self], mate())
     below = lambda ref, at: ref.at[..., pl.ds(at, 8), :]
 
     def row_copies(index, source, offset, sink):
@@ -268,7 +263,24 @@
     rows_two = row_copies(8, diffs, 8, diffs)
     cols_two = col_copies(10, pack_out_two, pack_in_two)
     start_all(rows_one)
+    keep_image.wait()
+
+    def flatten(at):
+        group = jnp.swapaxes(wide[:, pl.ds(pl.multiple_of(at + 8, 8), 8), :], 0, 1)
+        for row in range(8):
+            where = pl.multiple_of((at + row) * cols, cols)
+            full[own_rows, pl.ds(where, cols)] = group[row]
+
+    def flatten_part(which):
+        def body(step, carried):
+            flatten(pl.multiple_of(which * (rows // 2) + step * 8, 8))
+            return carried
+
+        lax.fori_loop(0, rows // 16, body, 0)
+
+    flatten_part(partner)
     first_part.start()
+    flatten_part(me)
 
     tall = rows + 16
     tile_lane = lax.broadcasted_iota(jnp.int32, (tall, 128), 1)
@@ -301,7 +313,6 @@
     valid = valid & (col_at >= 0) & (col_at < count["fcol"] * cols)
     inside = lambda values: jnp.where(valid, values, 0.0)
 
-    keep_image.wait()
     arrive_all(rows_one)
     pack_edges(lambda ch, at: wide[ch, :, at], pack_out.__setitem__)
     start_all(cols_one)
@@ -324,7 +335,6 @@
     lax.fori_loop(0, channels, analyse, 0)
     share_sums = copy_to(6, sums, other_sums, mate())
 
-    keep_flat.wait()
     first_part.wait_recv()
     order = 2 * channels
     block = 1024
@@ -429,7 +439,7 @@
             jax.ShapeDtypeStruct(image_cube.shape, f32),
             jax.ShapeDtypeStruct((channels, pixels), f32),
         ),
-        in_specs=[anywhere, anywhere, in_vmem],
+        in_specs=[anywhere, in_vmem],
         out_specs=(in_vmem, in_vmem),
         scratch_shapes=[
             pltpu.VMEM((channels, tall, cols), f32),
@@ -447,12 +457,12 @@
             pltpu.VMEM((2, 2, tall, 128), f32),
             pltpu.SemaphoreType.DMA((12,)),
             pltpu.SemaphoreType.DMA((12,)),
-            pltpu.SemaphoreType.DMA((2,)),
+            pltpu.SemaphoreType.DMA((1,)),
         ],
         compiler_params=pltpu.CompilerParams(
             collective_id=0, has_side_effects=True, vmem_limit_bytes=50 * 2**20
         ),
-    )(image_cube, image_cube.reshape(channels, pixels), weights)
+    )(image_cube, weights)
     return back, rank.reshape(image_cube.shape)
 
 

time: 57.7 us -> 57.5 us (level)
  local copies, waits for them, and re-layouts: 5.16 us -> 4.4 us
    unnamed x7 -> x6, local copies, waits for them, and re-layouts: 5.16 us -> 4.4 us
where the time goes in v2:
time: 57.5 us; the launch traced here: 57.3 us
  Pallas kernels  52.3 us (91%)
  local copies, waits for them, and re-layouts  4.4 us (8%)
  between operations  0.65 us (1%)
    pallas_call x1, Pallas kernels, shards(): pl.pallas_call(functools.partial(facet_kernel, threshold), out_shape=(jax...  52.3 us
    unnamed x6, local copies, waits for them, and re-layouts  4.4 us

profile of v2, /device:TPU:1, one launch (start us, length us, event | category | flops | bytes accessed | tf_op | source)
XLA Modules:
  0.0 57.3 jit_solution(12935196090828973606)
XLA Ops:
  0.6 0.0 copy-start
  0.6 1.2 %copy-done = f32[16,64,256]{2,1,0:T(8,128)S(1)} copy-done((f32[16,64,256]{2,1,0:T(8,128)S(1)}, f32[16,64,256]{2,1,0:T(8,128)}, u32[]{:S(2)}) %copy-start) | copy-done | bytes 1048600
  1.9 0.0 copy-start.1
  1.9 0.9 %copy-done.1 = f32[3,64,256]{2,1,0:T(8,128)S(1)} copy-done((f32[3,64,256]{2,1,0:T(8,128)S(1)}, f32[3,64,256]{2,1,0:T(8,128)}, u32[]{:S(2)}) %copy-start.1) | copy-done | bytes 196632
  2.8 52.3 %shard_map.41 = (f32[16,64,256]{2,1,0:T(8,128)S(1)}, f32[16,16384]{1,0:T(8,128)S(1)}) custom-call(f32[16,64,256]{2,1,0:T(8,128)S(1)} %copy-done, f32[3,64,256]{2,1,0:T(8,128)S(1)} %copy-done.1), custom_call_target="tpu_custom_call" | custom-call | tf_op jit(solution)/shard_map/pallas_call | solution.py:436
  55.1 1.3 %copy.4 = f32[2,8,64,256]{3,2,1,0:T(8,128)} copy(f32[2,8,64,256]{3,1,2,0:T(8,128)S(1)} %bitcast.2) | data formatting | bytes 2097152
  56.4 1.0 %copy.6 = f32[16,64,256]{2,1,0:T(8,128)} copy(f32[16,64,256]{2,1,0:T(8,128)S(1)} %get-tuple-element.8) | data formatting | bytes 2097152
Async XLA Ops:
  0.6 1.2 %copy-start = (f32[16,64,256]{2,1,0:T(8,128)S(1)}, f32[16,64,256]{2,1,0:T(8,128)}, u32[]{:S(2)}) copy-start(f32[16,64,256]{2,1,0:T(8,128)} %image_ref.1) | copy-start | bytes 3145732
  1.9 0.9 %copy-start.1 = (f32[3,64,256]{2,1,0:T(8,128)S(1)}, f32[3,64,256]{2,1,0:T(8,128)}, u32[]{:S(2)}) copy-start(f32[3,64,256]{2,1,0:T(8,128)} %weights_ref.1) | copy-start | bytes 589828

commit v3 on v2

--- a/solution.py
+++ b/solution.py
@@ -143,7 +143,7 @@
 
 def facet_kernel(
     threshold, image_ref, weights_ref, back_ref, rank_ref,
-    wide, bands, sums, other_sums, diffs, full, gram, other_gram, mixing,
+    weight_scratch, wide, bands, sums, other_sums, diffs, full, gram, other_gram, mixing,
     pack_out, pack_in, pack_out_two, pack_in_two, send_sems, recv_sems, local_sems,
 ):
     channels, rows, cols = image_ref.shape
@@ -179,11 +179,12 @@
 
     own_rows = pl.ds(pl.multiple_of(me * channels, channels), channels)
     to_mate = pl.ds(pl.multiple_of(partner * part, part), part)
-    to_self = pl.ds(pl.multiple_of(me * part, part), part)
     keep_image = pltpu.make_async_copy(
         image_ref, wide.at[:, pl.ds(8, rows), :], local_sems.at[0]
     )
+    keep_weights = pltpu.make_async_copy(weights_ref, weight_scratch, local_sems.at[1])
     keep_image.start()
+    keep_weights.start()
 
     zero_rows = jnp.zeros((channels, 8, cols), jnp.float32)
 
@@ -215,10 +216,13 @@
             pl.semaphore_signal(barrier, inc=1, device_id=target(*key), device_id_type=mesh_ids)
 
         friends = friends + jnp.where(has[key], 1, 0)
-    pl.semaphore_wait(barrier, friends)
 
     first_part = copy_to(0, full.at[own_rows, to_mate], full.at[own_rows, to_mate], mate())
-    second_part = copy_to(1, full.at[own_rows, to_self], full.at[own_rows, to_self], mate())
+    piece = part // 8
+    early = pl.ds(pl.multiple_of(me * part, piece), piece)
+    later = pl.ds(pl.multiple_of(me * part + piece, piece), part - piece)
+    early_part = copy_to(12, full.at[own_rows, early], full.at[own_rows, early], mate())
+    second_part = copy_to(1, full.at[own_rows, later], full.at[own_rows, later], mate())
     below = lambda ref, at: ref.at[..., pl.ds(at, 8), :]
 
     def row_copies(index, source, offset, sink):
@@ -262,7 +266,6 @@
     cols_one = col_copies(4, pack_out, pack_in)
     rows_two = row_copies(8, diffs, 8, diffs)
     cols_two = col_copies(10, pack_out_two, pack_in_two)
-    start_all(rows_one)
     keep_image.wait()
 
     def flatten(at):
@@ -279,8 +282,11 @@
         lax.fori_loop(0, rows // 16, body, 0)
 
     flatten_part(partner)
+    pl.semaphore_wait(barrier, friends)
     first_part.start()
+    start_all(rows_one)
     flatten_part(me)
+    early_part.start()
 
     tall = rows + 16
     tile_lane = lax.broadcasted_iota(jnp.int32, (tall, 128), 1)
@@ -365,8 +371,9 @@
     turn = lambda _, carried: rank_round(carried, marks)
     state = lax.fori_loop(0, 3 * rounds // 10, turn, state)
     share_sums.wait_recv()
+    keep_weights.wait()
     for index in range(3):
-        levels = band_levels[index] * weights_ref[index]
+        levels = band_levels[index] * weight_scratch[index]
         totals = sums[index] + other_sums[index]
         other_sums[index] = levels / jnp.sqrt(jnp.maximum(totals, levels * levels))
 
@@ -390,6 +397,20 @@
     state = lax.fori_loop(8 * rounds // 10, rounds, turn, state)
     mixing[:, :order] = rank_finish(state, marks, threshold)
 
+    high, low = split_two(mixing[own_rows, :order])
+    left = jnp.concatenate([high, high, low, low], axis=1)
+
+    def rank_part(which):
+        def body(step, carried):
+            at = pl.ds(pl.multiple_of(which * part + step * block, block), block)
+            high, low = split_two(full[:, at])
+            right = jnp.concatenate([high, low, high, low], axis=0)
+            rank_ref[:, at] = jnp.dot(left, right, preferred_element_type=jnp.float32)
+            return carried
+
+        lax.fori_loop(0, part // block, body, 0)
+
+    rank_part(me)
     arrive_all(cols_two)
 
     def synthesise(ch, carried):
@@ -406,21 +427,12 @@
 
     lax.fori_loop(0, channels, synthesise, 0)
 
+    early_part.wait_recv()
     second_part.wait_recv()
-    high, low = split_two(mixing[own_rows, :order])
-    left = jnp.concatenate([high, high, low, low], axis=1)
-
-    def rank_step(step, carried):
-        at = pl.ds(pl.multiple_of(step * block, block), block)
-        high, low = split_two(full[:, at])
-        right = jnp.concatenate([high, low, high, low], axis=0)
-        rank_ref[:, at] = jnp.dot(left, right, preferred_element_type=jnp.float32)
-        return carried
-
-    lax.fori_loop(0, pixels // block, rank_step, 0)
+    rank_part(partner)
     for copies in (rows_one, cols_one, rows_two, cols_two):
         left_all(copies)
-    for copy in (first_part, second_part, share_sums, share_gram):
+    for copy in (first_part, early_part, second_part, share_sums, share_gram):
         copy.wait_send()
 
 
@@ -431,7 +443,7 @@
     order = channels * lax.axis_size("chan")
     tall = rows + 16
     f32 = jnp.float32
-    anywhere = pl.BlockSpec(memory_space=pl.ANY)
+    far = pl.BlockSpec(memory_space=pltpu.HBM)
     in_vmem = pl.BlockSpec(memory_space=pltpu.VMEM)
     back, rank = pl.pallas_call(
         functools.partial(facet_kernel, threshold),
@@ -439,9 +451,10 @@
             jax.ShapeDtypeStruct(image_cube.shape, f32),
             jax.ShapeDtypeStruct((channels, pixels), f32),
         ),
-        in_specs=[anywhere, in_vmem],
+        in_specs=[far, far],
         out_specs=(in_vmem, in_vmem),
         scratch_shapes=[
+            pltpu.VMEM((3, rows, cols), f32),
             pltpu.VMEM((channels, tall, cols), f32),
             pltpu.VMEM((3, channels, rows, cols), f32),
             pltpu.VMEM((3, rows, cols), f32),
@@ -455,9 +468,9 @@
             pltpu.VMEM((2, tall, 128), f32),
             pltpu.VMEM((2, 2, tall, 128), f32),
             pltpu.VMEM((2, 2, tall, 128), f32),
-            pltpu.SemaphoreType.DMA((12,)),
-            pltpu.SemaphoreType.DMA((12,)),
-            pltpu.SemaphoreType.DMA((1,)),
+            pltpu.SemaphoreType.DMA((13,)),
+            pltpu.SemaphoreType.DMA((13,)),
+            pltpu.SemaphoreType.DMA((2,)),
         ],
         compiler_params=pltpu.CompilerParams(
             collective_id=0, has_side_effects=True, vmem_limit_bytes=50 * 2**20

time: 57.5 us -> 57.7 us (level)
  no operation moved by 1% of the time
where the time goes in v3:
time: 57.7 us; the launch traced here: 57.6 us
  Pallas kernels  52.5 us (91%)
  local copies, waits for them, and re-layouts  4.4 us (8%)
  between operations  0.65 us (1%)
    pallas_call x1, Pallas kernels, shards(): pl.pallas_call(functools.partial(facet_kernel, threshold), out_shape=(jax...  52.5 us
    unnamed x6, local copies, waits for them, and re-layouts  4.4 us

profile of v3, /device:TPU:1, one launch (start us, length us, event | category | flops | bytes accessed | tf_op | source)
XLA Modules:
  0.0 57.6 jit_solution(13965422365069628547)
XLA Ops:
  0.6 0.0 copy-start
  0.6 1.2 %copy-done = f32[16,64,256]{2,1,0:T(8,128)S(1)} copy-done((f32[16,64,256]{2,1,0:T(8,128)S(1)}, f32[16,64,256]{2,1,0:T(8,128)}, u32[]{:S(2)}) %copy-start) | copy-done | bytes 1048600
  1.9 0.0 copy-start.1
  1.9 0.9 %copy-done.1 = f32[3,64,256]{2,1,0:T(8,128)S(1)} copy-done((f32[3,64,256]{2,1,0:T(8,128)S(1)}, f32[3,64,256]{2,1,0:T(8,128)}, u32[]{:S(2)}) %copy-start.1) | copy-done | bytes 196632
  2.8 52.5 %shard_map.41 = (f32[16,64,256]{2,1,0:T(8,128)S(1)}, f32[16,16384]{1,0:T(8,128)S(1)}) custom-call(f32[16,64,256]{2,1,0:T(8,128)S(1)} %copy-done, f32[3,64,256]{2,1,0:T(8,128)S(1)} %copy-done.1), custom_call_target="tpu_custom_call" | custom-call | tf_op jit(solution)/shard_map/pallas_call | solution.py:448
  55.3 1.3 %copy.4 = f32[2,8,64,256]{3,2,1,0:T(8,128)} copy(f32[2,8,64,256]{3,1,2,0:T(8,128)S(1)} %bitcast.2) | data formatting | bytes 2097152
  56.6 1.0 %copy.6 = f32[16,64,256]{2,1,0:T(8,128)} copy(f32[16,64,256]{2,1,0:T(8,128)S(1)} %get-tuple-element.8) | data formatting | bytes 2097152
Async XLA Ops:
  0.6 1.2 %copy-start = (f32[16,64,256]{2,1,0:T(8,128)S(1)}, f32[16,64,256]{2,1,0:T(8,128)}, u32[]{:S(2)}) copy-start(f32[16,64,256]{2,1,0:T(8,128)} %image_ref.1) | copy-start | bytes 3145732
  1.9 0.9 %copy-start.1 = (f32[3,64,256]{2,1,0:T(8,128)S(1)}, f32[3,64,256]{2,1,0:T(8,128)}, u32[]{:S(2)}) copy-start(f32[3,64,256]{2,1,0:T(8,128)} %weights_ref.1) | copy-start | bytes 589828
